TPU v7x, 256 devices: a whole 4x4x8 slice. The times are simulated.
256 devices in a mesh: section: 2 (over core), srv: 32 (over x, z), tp: 4 (over y).
Axes of the slice: x: 4, y: 4, z: 8, core: 2. Of those that a mesh axis runs over, the one named last changes fastest.
Arguments:
- queries: bfloat16 [8192, 4096], P(('section', 'srv'), 'tp'), may hold values from -40 to 40
- keys: bfloat16 [8192, 512], P(('section', 'srv'), 'tp'), may hold values from -40 to 40
- values: bfloat16 [8192, 512], P(('section', 'srv'), 'tp'), may hold values from -6 to 6
- residual: bfloat16 [8192, 4096], P(('section', 'srv'), 'tp'), may hold values from -6 to 6
- out_weight: bfloat16 [4096, 4096], P('tp', ('section', 'srv')), may hold values from -0.1875 to 0.1875
- norm_gain: float32 [4096], P('tp'), may hold values from 0.25 to 1.75
- level_shift: float32 [8, 4096], P(None, 'tp'), may hold values from -3 to 3
- doc_lengths: int32 [2, 4], P('section'), may hold values from 1 to 128, 256 in all within a row
- noise_level: int32 [2, 4], P('section'), may hold values from 0 to 7
Outputs:
- normed: bfloat16 [8192, 4096], P(('section', 'srv'), 'tp')
Inputs may be any that keep to these rules, and one draw needn't show every extreme that they name: `doc_lengths`: each micro-batch's lengths sum to 256.
All inputs are finite; a program needn't handle non-finite values.
Results may differ from a plain program's by a relative error of at most 0.013.
Values may be sent and summed in bfloat16 or wider, within the bound.
A program may use at most 64 MiB of HBM per device.

v0:
```python
import functools

import jax
import jax.numpy as jnp
from jax import lax
from jax.experimental import pallas as pl
from jax.experimental.pallas import tpu as pltpu
from jax.sharding import PartitionSpec as P

D = 4096
HEAD = 128
BLK = 16
ROWS = 128
NX = 4
NZ = 8
NT = 4
MESH = pl.DeviceIdType.MESH
NEG = -1e30
LOG2E = 1.4426950408889634


def arrive(sem, ref):
    pltpu.make_async_copy(ref, ref, sem).wait()


def nt_dot(a, b):
    return lax.dot_general(a, b, (((1,), (1,)), ((), ())), preferred_element_type=jnp.float32)


def kernel(
    doc_in, noise_in, q_in, k_in, v_in, res_in, wt_in, gain_in, shift_in, out_ref,
    doc_ref, noise_ref, q_ref, res_ref, gain_ref, shift_ref,
    kv, w, bias, m_s, l_s, acc, ab, ob, rb, hid, sq,
    sin, skz, skx1, sxx, sk2, swx, swf, swb, swd, sa, so, ss,
    rkz, rk1, rk2, rwx, rw, rwd, ra, ro, rs,
):
    sec = lax.axis_index("section")
    i = lax.axis_index("srv")
    t = lax.axis_index("tp")
    x = i // NZ
    z = i % NZ
    sgn = 1 - 2 * sec

    def dev(dx=0, dz=0):
        return (sec, ((x + dx + NX) % NX) * NZ + (z + dz + 2 * NZ) % NZ, t)

    def zmod(a):
        return (a + 2 * NZ) % NZ

    def send(src, dst, s, r, to):
        pltpu.make_async_remote_copy(
            src_ref=src, dst_ref=dst, send_sem=s, recv_sem=r, device_id=to, device_id_type=MESH
        ).start()

    peers = [dev(dz=1), dev(dz=-1), dev(dz=2), dev(dz=-2), (1 - sec, i, t)]
    peers.append(dev(dx=2))
    for dx in (-1, 0, 1):
        for d in range(NT):
            if dx or d:
                peers.append((sec, ((x + dx + NX) % NX) * NZ + z, (t + d) % NT))
    barrier = pltpu.get_barrier_semaphore()
    for peer in peers:
        pl.semaphore_signal(barrier, inc=1, device_id=peer, device_id_type=MESH)
    loads = [
        pltpu.make_async_copy(src, dst, sin.at[n])
        for n, (src, dst) in enumerate((
            (k_in, kv.at[x, z, 0]),
            (v_in, kv.at[x, z, 1]),
            (wt_in, w.at[0, sec, z]),
            (doc_in, doc_ref),
            (noise_in, noise_ref),
            (q_in, q_ref),
            (gain_in, gain_ref),
            (shift_in, shift_ref),
            (res_in, res_ref),
        ))
    ]
    for load in loads:
        load.start()
    for load in loads[:3]:
        load.wait()
    pl.semaphore_wait(barrier, len(peers))

    def kv_along_x(zz):
        @pl.when(x < NX - 1)
        def _():
            send(kv.at[x, zz], kv.at[x, zz], skx1.at[zz], rk1.at[zz], dev(dx=1))

    def when_send(cond, zz, n, dz):
        @pl.when(cond)
        def _():
            send(kv.at[x - 2, zz], kv.at[x - 2, zz], sk2.at[n], rk2.at[zz], dev(dz=dz))

    def when_here(cond, zz):
        @pl.when(cond)
        def _():
            arrive(rk2.at[zz], kv.at[x - 2, zz])

    def need(zz, d):
        return (x >= 2) & (zmod(zz + d) < zz)

    def by_two(zz, side):
        return need(zz, 2 * side) | need(zz, 3 * side) | (need(zz, 4) & (sgn == side))

    def old_first():
        when_here(x >= 2, z)
        when_send(need(z, 1), z, 0, 1)
        when_send(need(z, -1), z, 1, -1)
        when_send(by_two(z, 1), z, 2, 2)
        when_send(by_two(z, -1), z, 3, -2)

    def old_second():
        for side in (1, -1):
            zz = zmod(z - 2 * side)
            when_here(by_two(zz, side), zz)
            when_send(need(zz, 3 * side), zz, 4 + (1 - side) // 2, side)
        zz = zmod(z - 2 * sgn)
        when_send(need(zz, 4), zz, 6, 2 * sgn)

    def old_last():
        for d in (1, -1, 3, -3, 4):
            zz = zmod(z - d)
            when_here(need(zz, d), zz)

    for n, dz in enumerate((1, -1, 2, -2)):
        send(kv.at[x, z], kv.at[x, z], skz.at[n], rkz.at[z], dev(dz=dz))
    kv_along_x(z)

    @pl.when(x < NX - 2)
    def _():
        send(kv.at[x, z], kv.at[x, z], sxx.at[0], rk2.at[z], dev(dx=2))

    def kv_here(dz):
        zz = zmod(z + dz)
        arrive(rkz.at[zz], kv.at[x, zz])
        return zz

    def across():
        send(w.at[0, sec, z], w.at[1, sec, z], swx.at[0], rwx.at[0], dev(dx=2))

    def own_out(cl):
        piece = w.at[cl, sec, z]
        if cl:
            arrive(rwx.at[0], piece)
        send(piece, piece, swf.at[cl, 0], rw.at[cl, z], dev(dz=sgn))
        send(piece, piece, swb.at[cl, 0], rw.at[cl, z], dev(dz=-sgn))
        send(piece, piece, swd.at[cl, z], rwd.at[cl, z], (1 - sec, i, t))

    def ring(cl, k):
        zf = zmod(z - sgn * k)
        piece = w.at[cl, sec, zf]
        arrive(rw.at[cl, zf], piece)
        if k <= 3:
            send(piece, piece, swf.at[cl, k], rw.at[cl, zf], dev(dz=sgn))
        send(piece, piece, swd.at[cl, zf], rwd.at[cl, zf], (1 - sec, i, t))
        if k <= 3:
            zb = zmod(z + sgn * k)
            piece = w.at[cl, sec, zb]
            arrive(rw.at[cl, zb], piece)
            if k <= 2:
                send(piece, piece, swb.at[cl, k], rw.at[cl, zb], dev(dz=-sgn))
            send(piece, piece, swd.at[cl, zb], rwd.at[cl, zb], (1 - sec, i, t))

    def near():
        kv_along_x(kv_here(-1))
        kv_along_x(kv_here(1))
        left = kv_here(-2)
        send(kv.at[x, left], kv.at[x, left], skz.at[4], rkz.at[left], dev(dz=1))
        right = kv_here(2)
        send(kv.at[x, right], kv.at[x, right], skz.at[5], rkz.at[right], dev(dz=-1))
        far = zmod(z - 2 * sgn)
        send(kv.at[x, far], kv.at[x, far], skz.at[6], rkz.at[far], dev(dz=2 * sgn))
        kv_along_x(left)
        kv_along_x(right)

    def distant():
        kv_along_x(kv_here(-3))
        kv_along_x(kv_here(3))
        kv_along_x(kv_here(4))

    def before():
        @pl.when(x >= 1)
        def _():
            def one(zz, c):
                arrive(rk1.at[zz], kv.at[x - 1, zz])
                return c

            lax.fori_loop(0, NZ, one, 0)

    def second(h):
        @pl.when(x >= 1)
        def _():
            unit(1, h)

    def rest_of(h):
        unit(0, h)

    across()
    own_out(0)
    for load in loads[3:5]:
        load.wait()
    row = i * ROWS + lax.broadcasted_iota(jnp.int32, (ROWS, 1), 0)
    starts, ends, at = [], [], jnp.int32(0)
    for d in range(4):
        starts.append(at)
        at = at + doc_ref[0, d] * BLK
        ends.append(at)
    member = [(row >= starts[d]) & (row < ends[d]) for d in range(4)]
    first = jnp.zeros((ROWS, 1), jnp.int32)
    for d in range(4):
        first = jnp.where(member[d], starts[d], first)
    limit = (row // BLK + 1) * BLK

    lane = lax.broadcasted_iota(jnp.int32, (ROWS, ROWS), 1)

    def home(zz):
        return jnp.where((zz <= z) | (x < 2), x, x - 2)

    bases = [home(zz) * NZ * ROWS + zz * ROWS for zz in range(NZ)]
    bases += [(x - 1) * NZ * ROWS + zz * ROWS for zz in range(NZ)]
    bases += [(x - 2) * NZ * ROWS + z * ROWS]
    for n, base in enumerate(bases):
        bias[:, n * ROWS : (n + 1) * ROWS] = jnp.where(
            (lane >= first - base) & (lane < limit - base), 0.0, NEG
        )

    for load in loads[5:]:
        load.wait()

    def unit(b, h):
        def cols(n):
            return pl.ds(pl.multiple_of((2 * h + n) * HEAD, HEAD), HEAD)

        q = jnp.concatenate([q_ref[:, cols(0)], q_ref[:, cols(1)]], axis=0)
        if b == 0:
            spots = [(home(zz), zz) for zz in range(NZ)]
            mask = bias[:, : NZ * ROWS]
        else:
            spots = [(x - 1, zz) for zz in range(NZ)] + [(jnp.maximum(x - 2, 0), z)]
            mask = bias[:, NZ * ROWS :]
        keys = jnp.concatenate([kv[xx, zz, 0] for xx, zz in spots], axis=0)
        vals = jnp.concatenate([kv[xx, zz, 1] for xx, zz in spots], axis=0)
        s = nt_dot(q, keys) * (HEAD ** -0.5 * LOG2E) + jnp.concatenate([mask, mask], axis=0)
        best = jnp.max(s, axis=1, keepdims=True)
        if b == 1:
            old = m_s[h][:, :1]
            best = jnp.maximum(best, old)
        p = jnp.exp2(s - best)
        total = jnp.sum(p, axis=1, keepdims=True)
        summed = jnp.dot(p.astype(jnp.bfloat16), vals, preferred_element_type=jnp.float32)
        if b == 1:
            alpha = jnp.exp2(old - best)
            total = total + alpha * l_s[h][:, :1]
            summed = summed + alpha * acc[h]
        m_s[h] = jnp.broadcast_to(best, (2 * ROWS, HEAD))
        l_s[h] = jnp.broadcast_to(total, (2 * ROWS, HEAD))
        acc[h] = summed

    def finish(h):
        second(h)
        done = (acc[h] / l_s[h]).astype(jnp.bfloat16)
        for n in range(2):
            ab[x, :, (2 * h + n) * HEAD : (2 * h + n + 1) * HEAD] = done[n * ROWS : (n + 1) * ROWS]
        piece = ab.at[x, :, pl.ds(2 * h * HEAD, 2 * HEAD)]
        for n, dx in enumerate((1, -1)):
            send(piece, piece, sa.at[h, n], ra.at[h, n], dev(dx=dx))

    def all_weights(cl):
        def one(zz, c):
            arrive(rwd.at[cl, zz], w.at[cl, 1 - sec, zz])
            return c

        lax.fori_loop(0, NZ, one, 0)

    def project(j):
        dx = (0, -1, 1, 0)[j]
        cl = j // 3
        xx = (x + dx + NX) % NX
        if dx:
            for h in range(4):
                arrive(ra.at[h, j - 1], ab.at[xx, :, pl.ds(2 * h * HEAD, 2 * HEAD)])
        for s2 in range(2):
            o = nt_dot(ab[xx], w[cl, s2].reshape(512, 1024))
            ob[j, s2] = o.astype(jnp.bfloat16)
            to = 2 * s2 + ((x + 2 * cl) % NX) // 2
            lo = x % 2
            if dx:
                send(ob.at[j, s2], rb.at[lo, t], so.at[j, s2], ro.at[lo, t], (sec, xx * NZ + z, to))
            else:
                @pl.when(to == t)
                def _():
                    pltpu.make_async_copy(ob.at[j, s2], rb.at[lo, t], ro.at[lo, t]).start()

                @pl.when(to != t)
                def _():
                    send(ob.at[j, s2], rb.at[lo, t], so.at[j, s2], ro.at[lo, t], (sec, i, to))

    near()
    old_first()
    ring(0,1)
    own_out(1)
    distant()
    old_second()
    ring(0,2)
    ring(1,1)
    old_last()
    rest_of(0)
    rest_of(1)
    ring(0,3)
    rest_of(2)
    rest_of(3)
    ring(1,2)
    before()
    finish(0)
    finish(1)
    ring(0,4)
    finish(2)
    finish(3)
    ring(1,3)
    all_weights(0)
    project(0)
    ring(1,4)
    project(1)
    project(2)
    all_weights(1)
    project(3)
    squares = jnp.zeros((ROWS, 128), jnp.float32)
    for lo in range(2):
        for ts in range(NT):
            arrive(ro.at[lo, ts], rb.at[lo, ts])
        for c in range(4):
            cols = slice(c * 128, c * 128 + 128)
            wide = slice(lo * 512 + c * 128, lo * 512 + c * 128 + 128)
            h = res_ref[:, wide].astype(jnp.float32)
            for ts in range(NT):
                h = h + rb[lo, ts, :, cols].astype(jnp.float32)
            hid[:, wide] = h
            squares = squares + h * h
    column = jnp.broadcast_to(jnp.sum(squares, axis=1, keepdims=True), (ROWS, 128))
    sq[t] = jnp.transpose(column)[:8]
    for n, d in enumerate((1, 2, 3)):
        send(sq.at[t], sq.at[t], ss.at[n], rs.at[n], (sec, i, (t + d) % NT))
    gains = []
    for d in range(4):
        gains.append(gain_ref[...] * (1.0 + shift_ref[pl.ds(noise_ref[0, d], 1), :]))
    for n in range(7):
        arrive(skz.at[n], kv.at[0, 0])

    def drain(zz, c):
        for cl in range(2):
            arrive(swd.at[cl, zz], w.at[0, 0, 0])

        @pl.when(x < NX - 1)
        def _():
            arrive(skx1.at[zz], kv.at[0, 0])

        return c

    lax.fori_loop(0, NZ, drain, 0)
    arrive(swx.at[0], w.at[0, 0, 0])
    for cl in range(2):
        for k in range(4):
            arrive(swf.at[cl, k], w.at[0, 0, 0])
        for k in range(3):
            arrive(swb.at[cl, k], w.at[0, 0, 0])
    for h in range(4):
        for n in range(2):
            arrive(sa.at[h, n], ab.at[0, :, pl.ds(0, 2 * HEAD)])
    for s2 in range(2):
        for cl in range(2):
            @pl.when(2 * s2 + ((x + 2 * cl) % NX) // 2 != t)
            def _():
                arrive(so.at[3 * cl, s2], rb.at[0, 0])

        for j in (1, 2):
            arrive(so.at[j, s2], rb.at[0, 0])

    @pl.when(x < NX - 2)
    def _():
        arrive(sxx.at[0], kv.at[0, 0])

    def sent(cond, n):
        @pl.when(cond)
        def _():
            arrive(sk2.at[n], kv.at[0, 0])

    sent(need(z, 1), 0)
    sent(need(z, -1), 1)
    sent(by_two(z, 1), 2)
    sent(by_two(z, -1), 3)
    sent(need(zmod(z - 2), 3), 4)
    sent(need(zmod(z + 2), -3), 5)
    sent(need(zmod(z - 2 * sgn), 4), 6)

    for n, d in enumerate((1, 2, 3)):
        arrive(rs.at[n], sq.at[(t - d + NT) % NT])
    for n in range(3):
        arrive(ss.at[n], sq.at[0])
    whole = sq[0] + sq[1] + sq[2] + sq[3]
    inverse = jnp.transpose(jnp.broadcast_to(lax.rsqrt(whole[:1] / D + 1e-6), (ROWS, 128)))
    for c in range(8):
        cols = slice(c * 128, c * 128 + 128)
        g = jnp.broadcast_to(gains[0][:, cols], (ROWS, 128))
        for d in range(1, 4):
            g = jnp.where(member[d], gains[d][:, cols], g)
        out_ref[:, cols] = (hid[:, cols] * inverse * g).astype(jnp.bfloat16)


def on_device(queries, keys, values, residual, out_weight, norm_gain, level_shift, doc_lengths, noise_level):
    bf, f32, sem = jnp.bfloat16, jnp.float32, pltpu.SemaphoreType.DMA
    vm = pl.BlockSpec(memory_space=pltpu.VMEM)
    hbm = pl.BlockSpec(memory_space=pltpu.MemorySpace.HBM)
    return pl.pallas_call(
        kernel,
        out_shape=jax.ShapeDtypeStruct((ROWS, 1024), bf),
        in_specs=[hbm] * 9,
        out_specs=vm,
        scratch_shapes=[
            pltpu.SMEM((1, 4), jnp.int32),
            pltpu.SMEM((1, 4), jnp.int32),
            pltpu.VMEM((ROWS, 1024), bf),
            pltpu.VMEM((ROWS, 1024), bf),
            pltpu.VMEM((1, 1024), f32),
            pltpu.VMEM((8, 1024), f32),
            pltpu.VMEM((NX, NZ, 2, ROWS, HEAD), bf),
            pltpu.VMEM((2, 2, NZ, 64, 1024), bf),
            pltpu.VMEM((ROWS, 17 * ROWS), f32),
            pltpu.VMEM((4, 2 * ROWS, HEAD), f32),
            pltpu.VMEM((4, 2 * ROWS, HEAD), f32),
            pltpu.VMEM((4, 2 * ROWS, HEAD), f32),
            pltpu.VMEM((NX, ROWS, 1024), bf),
            pltpu.VMEM((4, 2, ROWS, 512), bf),
            pltpu.VMEM((2, NT, ROWS, 512), bf),
            pltpu.VMEM((ROWS, 1024), f32),
            pltpu.VMEM((NT, 8, 128), f32),
            sem((9,)), sem((7,)), sem((NZ,)), sem((1,)), sem((7,)),
            sem((1,)), sem((2, 4)), sem((2, 3)), sem((2, NZ)), sem((4, 2)), sem((4, 2)), sem((3,)),
            sem((NZ,)), sem((NZ,)), sem((NZ,)),
            sem((1,)), sem((2, NZ)), sem((2, NZ)), sem((4, 2)), sem((2, NT)), sem((3,)),
        ],
        compiler_params=pltpu.CompilerParams(
            collective_id=0, has_side_effects=True, vmem_limit_bytes=64 << 20
        ),
    )(
        doc_lengths, noise_level, queries, keys, values, residual, out_weight.T,
        norm_gain.reshape(1, 1024), level_shift,
    )


def solution(mesh):
    placed = (
        P(("section", "srv"), "tp"),
        P(("section", "srv"), "tp"),
        P(("section", "srv"), "tp"),
        P(("section", "srv"), "tp"),
        P("tp", ("section", "srv")),
        P("tp"),
        P(None, "tp"),
        P("section", None),
        P("section", None),
    )
    return jax.shard_map(
        on_device,
        mesh=mesh,
        in_specs=placed,
        out_specs=P(("section", "srv"), "tp"),
        check_vma=False,
    )
```

profile of v0, /device:TPU:96, one launch (start us, length us, event | category | flops | bytes accessed | tf_op | source)
XLA Modules:
  0.0 69.5 jit_solution(13924594886800431685)
XLA Ops:
  0.0 67.8 %shard_map.91 = bf16[128,1024]{1,0:T(8,128)(2,1)} custom-call(s32[1,4]{1,0:T(1,128)} %doc_in.1, s32[1,4]{1,0:T(1,128)} %noise_in.1, bf16[128,1024]{1,0:T(8,128)(2,1)} %q_in.1, bf16[128,128]{1,0:T(8,128)(2,1)} %k_in.1, bf16[128,128]{1,0:T(8,128)(2,1)} %v_in.1, bf16[128,1024]{1,0:T(8,128)(2,1)} %res_in.1, bf16[64,1024]{1,0:T(8,128)(2,1)} %bitcast.2, ...), custom_call_target="tpu_custom_call" | custom-call | tf_op jit(solution)/shard_map/pallas_call | solution.py:413
  67.8 1.7 %copy.11 = bf16[128,1024]{1,0:T(8,128)(2,1)} copy(bf16[128,1024]{1,0:T(8,128)(2,1)} %shard_map.91) | data formatting | bytes 524288
where the time goes:
time: 69.6 us; the launch traced here: 69.5 us
  Pallas kernels  67.8 us (97%)
  local copies, waits for them, and re-layouts  1.67 us (2%)
    pallas_call x1, Pallas kernels, on_device(): pl.pallas_call(kernel, out_shape=jax.ShapeDtypeStruct((ROWS, 1024), bf),...  67.8 us
    unnamed x1, local copies, waits for them, and re-layouts  1.67 us

commit v1 on v0

--- a/solution.py
+++ b/solution.py
@@ -195,7 +195,6 @@
     def rest_of(h):
         unit(0, h)
 
-    across()
     own_out(0)
     for load in loads[3:5]:
         load.wait()
@@ -298,30 +297,31 @@
     near()
     old_first()
     ring(0,1)
-    own_out(1)
     distant()
+    across()
     old_second()
     ring(0,2)
-    ring(1,1)
+    own_out(1)
     old_last()
     rest_of(0)
     rest_of(1)
     ring(0,3)
     rest_of(2)
     rest_of(3)
-    ring(1,2)
+    ring(1,1)
     before()
     finish(0)
     finish(1)
     ring(0,4)
     finish(2)
     finish(3)
-    ring(1,3)
+    ring(1,2)
     all_weights(0)
     project(0)
-    ring(1,4)
+    ring(1,3)
     project(1)
     project(2)
+    ring(1,4)
     all_weights(1)
     project(3)
     squares = jnp.zeros((ROWS, 128), jnp.float32)

time: 69.6 us -> 68 us (0.977)
  the two profiles are of different devices: /device:TPU:96 before, /device:TPU:1 now
where the time goes in v1:
time: 68 us; the launch traced here: 67.9 us
  Pallas kernels  66.2 us (97%)
  local copies, waits for them, and re-layouts  1.67 us (2%)
    pallas_call x1, Pallas kernels, on_device(): pl.pallas_call(kernel, out_shape=jax.ShapeDtypeStruct((ROWS, 1024), bf),...  66.2 us
    unnamed x1, local copies, waits for them, and re-layouts  1.67 us

profile of v1, /device:TPU:1, one launch (start us, length us, event | category | flops | bytes accessed | tf_op | source)
XLA Modules:
  0.0 67.9 jit_solution(7485600096729851761)
XLA Ops:
  0.0 66.2 %shard_map.91 = bf16[128,1024]{1,0:T(8,128)(2,1)} custom-call(s32[1,4]{1,0:T(1,128)} %doc_in.1, s32[1,4]{1,0:T(1,128)} %noise_in.1, bf16[128,1024]{1,0:T(8,128)(2,1)} %q_in.1, bf16[128,128]{1,0:T(8,128)(2,1)} %k_in.1, bf16[128,128]{1,0:T(8,128)(2,1)} %v_in.1, bf16[128,1024]{1,0:T(8,128)(2,1)} %res_in.1, bf16[64,1024]{1,0:T(8,128)(2,1)} %bitcast.2, ...), custom_call_target="tpu_custom_call" | custom-call | tf_op jit(solution)/shard_map/pallas_call | solution.py:413
  66.2 1.7 %copy.11 = bf16[128,1024]{1,0:T(8,128)(2,1)} copy(bf16[128,1024]{1,0:T(8,128)(2,1)} %shard_map.91) | data formatting | bytes 524288

commit v2 on v1

--- a/solution.py
+++ b/solution.py
@@ -297,8 +297,8 @@
     near()
     old_first()
     ring(0,1)
+    across()
     distant()
-    across()
     old_second()
     ring(0,2)
     own_out(1)

time: 68 us -> 68 us (level)
  no operation moved by 1% of the time
where the time goes in v2:
time: 68 us; the launch traced here: 67.9 us
  Pallas kernels  66.2 us (97%)
  local copies, waits for them, and re-layouts  1.67 us (2%)
    pallas_call x1, Pallas kernels, on_device(): pl.pallas_call(kernel, out_shape=jax.ShapeDtypeStruct((ROWS, 1024), bf),...  66.2 us
    unnamed x1, local copies, waits for them, and re-layouts  1.67 us

profile of v2, /device:TPU:1, one launch (start us, length us, event | category | flops | bytes accessed | tf_op | source)
XLA Modules:
  0.0 67.9 jit_solution(6864222393383140560)
XLA Ops:
  0.0 66.2 %shard_map.91 = bf16[128,1024]{1,0:T(8,128)(2,1)} custom-call(s32[1,4]{1,0:T(1,128)} %doc_in.1, s32[1,4]{1,0:T(1,128)} %noise_in.1, bf16[128,1024]{1,0:T(8,128)(2,1)} %q_in.1, bf16[128,128]{1,0:T(8,128)(2,1)} %k_in.1, bf16[128,128]{1,0:T(8,128)(2,1)} %v_in.1, bf16[128,1024]{1,0:T(8,128)(2,1)} %res_in.1, bf16[64,1024]{1,0:T(8,128)(2,1)} %bitcast.2, ...), custom_call_target="tpu_custom_call" | custom-call | tf_op jit(solution)/shard_map/pallas_call | solution.py:413
  66.2 1.7 %copy.11 = bf16[128,1024]{1,0:T(8,128)(2,1)} copy(bf16[128,1024]{1,0:T(8,128)(2,1)} %shard_map.91) | data formatting | bytes 524288

commit v3 on v2

--- a/solution.py
+++ b/solution.py
@@ -32,7 +32,7 @@
     doc_ref, noise_ref, q_ref, res_ref, gain_ref, shift_ref,
     kv, w, bias, m_s, l_s, acc, ab, ob, rb, hid, sq,
     sin, skz, skx1, sxx, sk2, swx, swf, swb, swd, sa, so, ss,
-    rkz, rk1, rk2, rwx, rw, rwd, ra, ro, rs,
+    result, sout, rkz, rk1, rk2, rwx, rw, rwd, ra, ro, rs,
 ):
     sec = lax.axis_index("section")
     i = lax.axis_index("srv")
@@ -398,12 +398,19 @@
         arrive(ss.at[n], sq.at[0])
     whole = sq[0] + sq[1] + sq[2] + sq[3]
     inverse = jnp.transpose(jnp.broadcast_to(lax.rsqrt(whole[:1] / D + 1e-6), (ROWS, 128)))
+    stores = []
     for c in range(8):
         cols = slice(c * 128, c * 128 + 128)
         g = jnp.broadcast_to(gains[0][:, cols], (ROWS, 128))
         for d in range(1, 4):
             g = jnp.where(member[d], gains[d][:, cols], g)
-        out_ref[:, cols] = (hid[:, cols] * inverse * g).astype(jnp.bfloat16)
+        result[:, cols] = (hid[:, cols] * inverse * g).astype(jnp.bfloat16)
+        if c % 4 == 3:
+            block = slice(c * 128 - 384, c * 128 + 128)
+            stores.append(pltpu.make_async_copy(result.at[:, block], out_ref.at[:, block], sout.at[c // 4]))
+            stores[-1].start()
+    for store in stores:
+        store.wait()
 
 
 def on_device(queries, keys, values, residual, out_weight, norm_gain, level_shift, doc_lengths, noise_level):
@@ -414,7 +421,7 @@
         kernel,
         out_shape=jax.ShapeDtypeStruct((ROWS, 1024), bf),
         in_specs=[hbm] * 9,
-        out_specs=vm,
+        out_specs=hbm,
         scratch_shapes=[
             pltpu.SMEM((1, 4), jnp.int32),
             pltpu.SMEM((1, 4), jnp.int32),
@@ -435,7 +442,7 @@
             pltpu.VMEM((NT, 8, 128), f32),
             sem((9,)), sem((7,)), sem((NZ,)), sem((1,)), sem((7,)),
             sem((1,)), sem((2, 4)), sem((2, 3)), sem((2, NZ)), sem((4, 2)), sem((4, 2)), sem((3,)),
-            sem((NZ,)), sem((NZ,)), sem((NZ,)),
+            pltpu.VMEM((ROWS, 1024), bf), sem((2,)), sem((NZ,)), sem((NZ,)), sem((NZ,)),
             sem((1,)), sem((2, NZ)), sem((2, NZ)), sem((4, 2)), sem((2, NT)), sem((3,)),
         ],
         compiler_params=pltpu.CompilerParams(

time: 68 us -> 68 us (level)
  no operation moved by 1% of the time
where the time goes in v3:
time: 68 us; the launch traced here: 67.9 us
  Pallas kernels  66.2 us (97%)
  local copies, waits for them, and re-layouts  1.67 us (2%)
    pallas_call x1, Pallas kernels, on_device(): pl.pallas_call(kernel, out_shape=jax.ShapeDtypeStruct((ROWS, 1024), bf),...  66.2 us
    unnamed x1, local copies, waits for them, and re-layouts  1.67 us

profile of v3, /device:TPU:1, one launch (start us, length us, event | category | flops | bytes accessed | tf_op | source)
XLA Modules:
  0.0 67.9 jit_solution(9563228605661076260)
XLA Ops:
  0.0 66.2 %shard_map.91 = bf16[128,1024]{1,0:T(8,128)(2,1)} custom-call(s32[1,4]{1,0:T(1,128)} %doc_in.1, s32[1,4]{1,0:T(1,128)} %noise_in.1, bf16[128,1024]{1,0:T(8,128)(2,1)} %q_in.1, bf16[128,128]{1,0:T(8,128)(2,1)} %k_in.1, bf16[128,128]{1,0:T(8,128)(2,1)} %v_in.1, bf16[128,1024]{1,0:T(8,128)(2,1)} %res_in.1, bf16[64,1024]{1,0:T(8,128)(2,1)} %bitcast.2, ...), custom_call_target="tpu_custom_call" | custom-call | tf_op jit(solution)/shard_map/pallas_call | solution.py:420
  66.2 1.7 %copy.11 = bf16[128,1024]{1,0:T(8,128)(2,1)} copy(bf16[128,1024]{1,0:T(8,128)(2,1)} %shard_map.91) | data formatting | bytes 524288
